TPU v7x, 32 devices: a whole 2x2x4 slice. The times are simulated.
32 devices in a mesh: seq: 2 (over x), fsdp: 16 (over z, y, core).
Axes of the slice: x: 2, y: 2, z: 4, core: 2. Of those that a mesh axis runs over, the one named last changes fastest.
Arguments:
- tokens: bfloat16 [16, 1024, 768], P('fsdp', 'seq'), may hold values from -6 to 6
- prior_logits: bfloat16 [16, 12, 1024, 1024], P('fsdp', 'seq'), may hold values from -6 to 6
- lengths: int32 [16], P('fsdp'), may hold values from 256 to 1024, as said below
- order: int32 [16, 1024], P('fsdp'), may hold values from 0 to 1023, each once within a row
- cotangent: bfloat16 [16, 1024, 768], P('fsdp', 'seq'), may hold values from -6 to 6
- w_qkv: bfloat16 [768, 2304], P('fsdp'), may hold values from -0.21875 to 0.21875
- w_out: bfloat16 [768, 768], P('fsdp'), may hold values from -3.5 to 3.5
- w_in: bfloat16 [768, 3072], P('fsdp'), may hold values from -0.21875 to 0.21875
- w_back: bfloat16 [3072, 768], P('fsdp'), may hold values from -0.109375 to 0.109375
- bias_q: bfloat16 [768], P('fsdp'), may hold values from -1.5 to 1.5
- bias_v: bfloat16 [768], P('fsdp'), may hold values from -0.25 to 0.25
- bias_o: bfloat16 [768], P('fsdp'), may hold values from -1.5 to 1.5
- gain_one: bfloat16 [768], P('fsdp'), may hold values from 0.5 to 1.5
- shift_one: bfloat16 [768], P('fsdp'), may hold values from -1.5 to 1.5
- bias_in: bfloat16 [3072], P('fsdp'), may hold values from -1.5 to 1.5
- bias_back: bfloat16 [768], P('fsdp'), may hold values from -1.5 to 1.5
- gain_two: bfloat16 [768], P('fsdp'), may hold values from 0.5 to 1.5
- shift_two: bfloat16 [768], P('fsdp'), may hold values from -1.5 to 1.5
Outputs:
- output: bfloat16 [16, 1024, 768], P('fsdp', 'seq')
- raw_logits: bfloat16 [16, 12, 1024, 1024], P('fsdp', 'seq')
- tokens_grad: bfloat16 [16, 1024, 768], P('fsdp', 'seq')
- prior_grad: bfloat16 [16, 12, 1024, 1024], P('fsdp', 'seq')
- grad_w_qkv: float32 [768, 2304], P('fsdp')
- grad_w_out: float32 [768, 768], P('fsdp')
- grad_w_in: float32 [768, 3072], P('fsdp')
- grad_w_back: float32 [3072, 768], P('fsdp')
- grad_bias_q: float32 [768], P('fsdp')
- grad_bias_v: float32 [768], P('fsdp')
- grad_bias_o: float32 [768], P('fsdp')
- grad_gain_one: float32 [768], P('fsdp')
- grad_shift_one: float32 [768], P('fsdp')
- grad_bias_in: float32 [3072], P('fsdp')
- grad_bias_back: float32 [768], P('fsdp')
- grad_gain_two: float32 [768], P('fsdp')
- grad_shift_two: float32 [768], P('fsdp')
- rms: float32 [3], replicated
Inputs may be any that keep to these rules, and one draw needn't show every extreme that they name: `lengths`: positions below a sequence's length hold its tokens, the others are padding; some sequence has exactly 1024.
All inputs are finite; a program needn't handle non-finite values.
Results may differ from a plain program's by a relative error of at most 0.017.
Values may be sent and summed in bfloat16 or wider, within the bound.
No kernel may reach another device: no remote copies, remote signals or barrier semaphores. Data moves between devices by JAX's collectives and lax.ppermute only.
A program may use at most 192 MiB of HBM per device.

v0:
```python
import math

import jax
import jax.numpy as jnp
from jax import lax
from jax.sharding import PartitionSpec as P

HD = 64


eps_norm = 1e-05
masked_fill = -1e30


def layer_norm(values, gain, shift):
    average = jnp.mean(values, axis=-1, keepdims=True)
    centered = values - average
    variance = jnp.mean(centered * centered, axis=-1, keepdims=True)
    return centered * lax.rsqrt(variance + eps_norm) * gain + shift


def gelu_exact(values):
    return jax.nn.gelu(values, approximate=False)


def contract_rows(left, right):
    return lax.dot_general(
        left, right, (((0,), (0,)), ((), ())), preferred_element_type=jnp.float32
    )


def contract_cols(left, right):
    return lax.dot_general(
        left, right, (((1,), (1,)), ((), ())), preferred_element_type=jnp.float32
    )


def body(
    tokens,
    prior_logits,
    lengths,
    order,
    cotangent,
    w_qkv,
    w_out,
    w_in,
    w_back,
    bias_q,
    bias_v,
    bias_o,
    gain_one,
    shift_one,
    bias_in,
    bias_back,
    gain_two,
    shift_two,
):
    seq_count = lax.axis_size("seq")
    seq_index = lax.axis_index("seq")
    qkv_weight, proj_weight, query_bias, value_bias, proj_bias, first_gain, first_shift = (
        lax.all_gather(w_qkv, "fsdp", axis=0, tiled=True),
        lax.all_gather(w_out, "fsdp", axis=0, tiled=True),
        lax.all_gather(bias_q, "fsdp", axis=0, tiled=True),
        lax.all_gather(bias_v, "fsdp", axis=0, tiled=True),
        lax.all_gather(bias_o, "fsdp", axis=0, tiled=True),
        lax.all_gather(gain_one, "fsdp", axis=0, tiled=True),
        lax.all_gather(shift_one, "fsdp", axis=0, tiled=True),
    )
    rows = tokens[0]
    local_count = rows.shape[0]
    width = rows.shape[1]
    heads_local = prior_logits.shape[1]
    local_width = heads_local * HD
    total = local_count * seq_count
    scale = 1.0 / math.sqrt(HD)
    joint_bias = jnp.concatenate(
        [
            query_bias.astype(jnp.float32),
            jnp.zeros((width,), jnp.float32),
            value_bias.astype(jnp.float32),
        ]
    )
    joint = (jnp.dot(rows, qkv_weight, preferred_element_type=jnp.float32) + joint_bias).astype(
        jnp.bfloat16
    )
    joint = joint.reshape(local_count, 3, seq_count, local_width)
    headed = lax.all_to_all(joint, "seq", split_axis=2, concat_axis=0, tiled=True).reshape(
        total, 3, local_width
    )
    order_row = order[0]
    length = lengths[0]
    positions = jnp.arange(total, dtype=jnp.int32)
    inverse = jnp.zeros((total,), jnp.int32).at[order_row].set(positions)
    placed = headed[inverse]
    query_pos = placed[:, 0].reshape(total, heads_local, HD)
    key_pos = placed[:, 1].reshape(total, heads_local, HD)
    value_pos = placed[:, 2].reshape(total, heads_local, HD)
    key_valid = (positions < length)[None, None, :]
    prior = prior_logits[0]
    block = min(512, total)
    block_count = total // block

    def block_scores(start):
        query_blk = lax.dynamic_slice_in_dim(query_pos, start, block, 0)
        prior_blk = lax.dynamic_slice_in_dim(prior, start, block, 1).astype(jnp.float32)
        scores = (
            jnp.einsum("qhd,khd->hqk", query_blk, key_pos, preferred_element_type=jnp.float32)
            * scale
            + prior_blk
        )
        return (query_blk, scores)

    def forward_block(block_index, carry):
        raw_buf, context_buf, lse_buf = carry
        start = block_index * block
        query_blk, scores = block_scores(start)
        masked = jnp.where(key_valid, scores, masked_fill)
        largest = jnp.max(masked, axis=-1, keepdims=True)
        exponent = jnp.exp(masked - largest)
        row_total = jnp.sum(exponent, axis=-1, keepdims=True)
        weights = (exponent / row_total).astype(jnp.bfloat16)
        context_blk = jnp.einsum(
            "hqk,khd->qhd", weights, value_pos, preferred_element_type=jnp.float32
        ).astype(jnp.bfloat16)
        raw_buf = lax.dynamic_update_slice_in_dim(raw_buf, scores.astype(jnp.bfloat16), start, 1)
        context_buf = lax.dynamic_update_slice_in_dim(context_buf, context_blk, start, 0)
        lse_buf = lax.dynamic_update_slice_in_dim(lse_buf, largest + jnp.log(row_total), start, 1)
        return (raw_buf, context_buf, lse_buf)

    raw_buf, context_pos, lse_buf = lax.fori_loop(
        0,
        block_count,
        forward_block,
        (
            jnp.zeros((heads_local, total, total), jnp.bfloat16),
            jnp.zeros((total, heads_local, HD), jnp.bfloat16),
            jnp.zeros((heads_local, total, 1), jnp.float32),
        ),
    )
    context_stored = context_pos.reshape(total, local_width)[order_row].reshape(
        total, 1, local_width
    )
    context = lax.all_to_all(
        context_stored, "seq", split_axis=0, concat_axis=1, tiled=True
    ).reshape(local_count, width)
    attended = jnp.dot(context, proj_weight, preferred_element_type=jnp.float32) + proj_bias.astype(
        jnp.float32
    )
    tokens_f = rows.astype(jnp.float32)
    residual_one = tokens_f + attended
    hidden, norm_back_one = jax.vjp(
        layer_norm, residual_one, first_gain.astype(jnp.float32), first_shift.astype(jnp.float32)
    )
    hidden_low = hidden.astype(jnp.bfloat16)
    inner_weight, outer_weight, inner_bias, outer_bias, second_gain, second_shift = (
        lax.all_gather(w_in, "fsdp", axis=0, tiled=True),
        lax.all_gather(w_back, "fsdp", axis=0, tiled=True),
        lax.all_gather(bias_in, "fsdp", axis=0, tiled=True),
        lax.all_gather(bias_back, "fsdp", axis=0, tiled=True),
        lax.all_gather(gain_two, "fsdp", axis=0, tiled=True),
        lax.all_gather(shift_two, "fsdp", axis=0, tiled=True),
    )
    inner = jnp.dot(
        hidden_low, inner_weight, preferred_element_type=jnp.float32
    ) + inner_bias.astype(jnp.float32)
    activated_f, gelu_back = jax.vjp(gelu_exact, inner)
    activated = activated_f.astype(jnp.bfloat16)
    branch = jnp.dot(
        activated, outer_weight, preferred_element_type=jnp.float32
    ) + outer_bias.astype(jnp.float32)
    residual_two = hidden + branch
    normed_two, norm_back_two = jax.vjp(
        layer_norm, residual_two, second_gain.astype(jnp.float32), second_shift.astype(jnp.float32)
    )
    local_order = lax.dynamic_slice_in_dim(order_row, seq_index * local_count, local_count)
    valid_rows = (local_order < length).astype(jnp.float32)[:, None]
    sum_tokens, sum_attended, sum_branch, token_count = lax.psum(
        (
            jnp.sum(valid_rows * tokens_f * tokens_f),
            jnp.sum(valid_rows * attended * attended),
            jnp.sum(valid_rows * branch * branch),
            jnp.sum(valid_rows),
        ),
        ("seq", "fsdp"),
    )
    rms = jnp.sqrt(jnp.stack([sum_tokens, sum_attended, sum_branch]) / (token_count * width))
    d_output = cotangent[0].astype(jnp.float32) * valid_rows
    d_res_two, grad_gain_two, grad_shift_two = norm_back_two(d_output)
    d_branch = d_res_two.astype(jnp.bfloat16)
    grad_bias_back = jnp.sum(d_branch.astype(jnp.float32), axis=0)
    grad_w_back = contract_rows(activated, d_branch)
    d_activated = contract_cols(d_branch, outer_weight)
    d_inner = gelu_back(d_activated)[0].astype(jnp.bfloat16)
    grad_bias_in = jnp.sum(d_inner.astype(jnp.float32), axis=0)
    grad_w_in = contract_rows(hidden_low, d_inner)
    d_hidden = d_res_two + contract_cols(d_inner, inner_weight)
    d_res_one, grad_gain_one, grad_shift_one = norm_back_one(d_hidden)
    d_attended = d_res_one.astype(jnp.bfloat16)
    grad_bias_o = jnp.sum(d_attended.astype(jnp.float32), axis=0)
    grad_w_out = contract_rows(context, d_attended)
    d_context = contract_cols(d_attended, proj_weight).astype(jnp.bfloat16)
    d_context = d_context.reshape(local_count, seq_count, local_width)
    d_context_all = lax.all_to_all(
        d_context, "seq", split_axis=1, concat_axis=0, tiled=True
    ).reshape(total, local_width)
    d_context_pos = d_context_all[inverse].reshape(total, heads_local, HD)

    def backward_block(block_index, carry):
        dprior_buf, dquery_buf, dkey_acc, dvalue_acc = carry
        start = block_index * block
        query_blk, scores = block_scores(start)
        masked = jnp.where(key_valid, scores, masked_fill)
        lse_blk = lax.dynamic_slice_in_dim(lse_buf, start, block, 1)
        probability = jnp.exp(masked - lse_blk)
        weights = probability.astype(jnp.bfloat16)
        dcontext_blk = lax.dynamic_slice_in_dim(d_context_pos, start, block, 0)
        d_prob = jnp.einsum(
            "qhd,khd->hqk", dcontext_blk, value_pos, preferred_element_type=jnp.float32
        )
        row_term = jnp.sum(probability * d_prob, axis=-1, keepdims=True)
        d_scores = (probability * (d_prob - row_term)).astype(jnp.bfloat16)
        dprior_buf = lax.dynamic_update_slice_in_dim(dprior_buf, d_scores, start, 1)
        dquery_blk = (
            jnp.einsum("hqk,khd->qhd", d_scores, key_pos, preferred_element_type=jnp.float32)
            * scale
        )
        dquery_buf = lax.dynamic_update_slice_in_dim(dquery_buf, dquery_blk, start, 0)
        dkey_acc = (
            dkey_acc
            + jnp.einsum("hqk,qhd->khd", d_scores, query_blk, preferred_element_type=jnp.float32)
            * scale
        )
        dvalue_acc = dvalue_acc + jnp.einsum(
            "hqk,qhd->khd", weights, dcontext_blk, preferred_element_type=jnp.float32
        )
        return (dprior_buf, dquery_buf, dkey_acc, dvalue_acc)

    dprior_buf, dquery_buf, dkey_acc, dvalue_acc = lax.fori_loop(
        0,
        block_count,
        backward_block,
        (
            jnp.zeros((heads_local, total, total), jnp.bfloat16),
            jnp.zeros((total, heads_local, HD), jnp.float32),
            jnp.zeros((total, heads_local, HD), jnp.float32),
            jnp.zeros((total, heads_local, HD), jnp.float32),
        ),
    )
    d_joint_pos = jnp.stack(
        [
            dquery_buf.reshape(total, local_width),
            dkey_acc.reshape(total, local_width),
            dvalue_acc.reshape(total, local_width),
        ],
        axis=1,
    ).astype(jnp.bfloat16)
    d_joint_stored = d_joint_pos[order_row].reshape(total, 3, 1, local_width)
    d_joint = lax.all_to_all(
        d_joint_stored, "seq", split_axis=0, concat_axis=2, tiled=True
    ).reshape(local_count, 3 * width)
    grad_bias_q = jnp.sum(d_joint[:, :width].astype(jnp.float32), axis=0)
    grad_bias_v = jnp.sum(d_joint[:, 2 * width :].astype(jnp.float32), axis=0)
    grad_w_qkv = contract_rows(rows, d_joint)
    tokens_grad = (d_res_one + contract_cols(d_joint, qkv_weight)).astype(jnp.bfloat16)
    (
        pair_qkv,
        pair_out,
        pair_in,
        pair_back,
        pair_bias_q,
        pair_bias_v,
        pair_bias_o,
        pair_gain_one,
        pair_shift_one,
        pair_bias_in,
        pair_bias_back,
        pair_gain_two,
        pair_shift_two,
    ) = (
        lax.psum(grad_w_qkv.astype(jnp.bfloat16), "seq").astype(jnp.float32),
        lax.psum(grad_w_out.astype(jnp.bfloat16), "seq").astype(jnp.float32),
        lax.psum(grad_w_in.astype(jnp.bfloat16), "seq").astype(jnp.float32),
        lax.psum(grad_w_back.astype(jnp.bfloat16), "seq").astype(jnp.float32),
        lax.psum(grad_bias_q.astype(jnp.bfloat16), "seq").astype(jnp.float32),
        lax.psum(grad_bias_v.astype(jnp.bfloat16), "seq").astype(jnp.float32),
        lax.psum(grad_bias_o.astype(jnp.bfloat16), "seq").astype(jnp.float32),
        lax.psum(grad_gain_one.astype(jnp.bfloat16), "seq").astype(jnp.float32),
        lax.psum(grad_shift_one.astype(jnp.bfloat16), "seq").astype(jnp.float32),
        lax.psum(grad_bias_in.astype(jnp.bfloat16), "seq").astype(jnp.float32),
        lax.psum(grad_bias_back.astype(jnp.bfloat16), "seq").astype(jnp.float32),
        lax.psum(grad_gain_two.astype(jnp.bfloat16), "seq").astype(jnp.float32),
        lax.psum(grad_shift_two.astype(jnp.bfloat16), "seq").astype(jnp.float32),
    )
    owned = (
        lax.psum_scatter(pair_qkv, "fsdp", scatter_dimension=0, tiled=True),
        lax.psum_scatter(pair_out, "fsdp", scatter_dimension=0, tiled=True),
        lax.psum_scatter(pair_in, "fsdp", scatter_dimension=0, tiled=True),
        lax.psum_scatter(pair_back, "fsdp", scatter_dimension=0, tiled=True),
        lax.psum_scatter(pair_bias_q, "fsdp", scatter_dimension=0, tiled=True),
        lax.psum_scatter(pair_bias_v, "fsdp", scatter_dimension=0, tiled=True),
        lax.psum_scatter(pair_bias_o, "fsdp", scatter_dimension=0, tiled=True),
        lax.psum_scatter(pair_gain_one, "fsdp", scatter_dimension=0, tiled=True),
        lax.psum_scatter(pair_shift_one, "fsdp", scatter_dimension=0, tiled=True),
        lax.psum_scatter(pair_bias_in, "fsdp", scatter_dimension=0, tiled=True),
        lax.psum_scatter(pair_bias_back, "fsdp", scatter_dimension=0, tiled=True),
        lax.psum_scatter(pair_gain_two, "fsdp", scatter_dimension=0, tiled=True),
        lax.psum_scatter(pair_shift_two, "fsdp", scatter_dimension=0, tiled=True),
    )
    return (
        normed_two.astype(jnp.bfloat16)[None],
        raw_buf[None],
        tokens_grad[None],
        dprior_buf[None],
        owned[0],
        owned[1],
        owned[2],
        owned[3],
        owned[4],
        owned[5],
        owned[6],
        owned[7],
        owned[8],
        owned[9],
        owned[10],
        owned[11],
        owned[12],
        rms,
    )


def solution(mesh):
    return jax.shard_map(
        body,
        mesh=mesh,
        in_specs=(
            P("fsdp", "seq", None),
            P("fsdp", "seq", None, None),
            P("fsdp"),
            P("fsdp", None),
            P("fsdp", "seq", None),
            P("fsdp", None),
            P("fsdp", None),
            P("fsdp", None),
            P("fsdp", None),
            P("fsdp"),
            P("fsdp"),
            P("fsdp"),
            P("fsdp"),
            P("fsdp"),
            P("fsdp"),
            P("fsdp"),
            P("fsdp"),
            P("fsdp"),
        ),
        out_specs=(
            P("fsdp", "seq", None),
            P("fsdp", "seq", None, None),
            P("fsdp", "seq", None),
            P("fsdp", "seq", None, None),
            P("fsdp", None),
            P("fsdp", None),
            P("fsdp", None),
            P("fsdp", None),
            P("fsdp"),
            P("fsdp"),
            P("fsdp"),
            P("fsdp"),
            P("fsdp"),
            P("fsdp"),
            P("fsdp"),
            P("fsdp"),
            P("fsdp"),
            P(),
        ),
        check_vma=False,
    )
```

profile of v0, /device:TPU:0, one launch (start us, length us, event | category | flops | bytes accessed | tf_op | source)
XLA Modules:
  0.0 1158.3 jit_solution(11270746098248359767)
XLA Ops:
  19.6 63.9 %all-reduce.20 = (bf16[768]{0:T(1024)(128)(2,1)S(1)}, bf16[768]{0:T(1024)(128)(2,1)S(1)}, bf16[768]{0:T(1024)(128)(2,1)}, bf16[768]{0:T(1024)(128)(2,1)}, bf16[7...) all-reduce(bf16[768]{0:T(1024)(128)(2,1)S(1)} %dynamic-update-slice, ...), channel_id=1, replica_groups=mesh['seq'=2,'fsdp'=16] {'fsdp'}, use_global_device_ids=true, to_apply=%add.1 | all-reduce | flops 9216 | bytes 36864
  105.4 17.6 %all-to-all-done = bf16[512,3,2,384]{3,0,1,2:T(8,128)(2,1)S(1)} async-done(((bf16[512,3,2,384]{3,0,1,2:T(8,128)(2,1)}), bf16[512,3,2,384]{3,0,1,2:T(8,128)(2,1)S(1)}, u32[]{:S(2)}, u32[]{:S(2)}) %all-to-all-start) | async-done | bytes 2359328 | tf_op jit(solution)/shard_map/all_to_all | solution.py:87
  126.9 6.9 gather_fusion
  149.3 6.4 broadcast.174.clone
  155.7 31.1 %while.38 = (s32[]{:T(128)}, bf16[6,1024,1024]{2,1,0:T(8,128)(2,1)}, bf16[1024,6,64]{0,2,1:T(8,128)(2,1)S(1)}, f32[6,1024,1]{1,0,2:T(8,128)S(1)}, bf16[1024,6,64...) while((s32[]{:T(128)}, ...), condition=%wide.region_4.5_spmd.clone, body=%wide.region_1.4_spmd.clone.sunk | while | flops 846395392 | bytes 65397944 | solution.py:130
  156.4 7.3 convert_dynamic-update-slice_fusion.2
  171.9 7.4 convert_dynamic-update-slice_fusion.2
  201.0 6.5 all-to-all-done.1
  216.4 19.9 %multiply_convert_fusion.1 = (bf16[512,3072]{1,0:T(8,128)(2,1)}, f32[512,3072]{1,0:T(8,128)}, f32[512,3072]{1,0:T(8,128)}) fusion(f32[3072]{0:T(1024)S(1)} %convert_element_type.217, bf16[768,3072]{1,0:T(8,128)(2,1)} %all-gather.9.cloned.1.call-done, f32[512,768]{1,0:T(8,128)S(1)} %get-tuple-element.679, f32[768]{0:T(1024)S(1)} %convert_element_type.215, ...), kind=kOutput, calls=%fused_computation.47 | convolution fusion | flops 2521694208 | bytes 22042624 | tf_op jit(solution)/shard_map/dot_general | solution.py:163
  247.7 8.6 fusion.61
  267.0 7.9 all-to-all-done.2
  283.4 6.4 broadcast.174
  289.8 65.8 %while.39 = (s32[]{:T(128)}, bf16[6,1024,1024]{2,1,0:T(8,128)(2,1)}, bf16[1024,6,64]{0,2,1:T(8,128)(2,1)}, f32[1024,6,64]{0,2,1:T(8,128)S(1)}, f32[1024,6,64]{0,...) while((s32[]{:T(128)}, ...), condition=%wide.region_15.16_spmd.clone, body=%wide.region_13.0_spmd.clone.sunk | while | flops 2050029568 | bytes 127470920 | solution.py:238
  293.6 9.4 multiply_reduce_fusion.6
  303.0 7.0 bitcast_add_fusion.5
  310.0 8.9 constant_dynamic-update-slice_fusion.2
  326.3 9.5 multiply_reduce_fusion.6
  335.8 7.4 bitcast_add_fusion.5
  343.2 8.9 constant_dynamic-update-slice_fusion.2
  366.2 6.8 pad_maximum_fusion
  373.0 10.2 gather_fusion.3
  390.5 7.0 convolution_convert_fusion
  402.5 13.4 %all-to-all-done.3 = bf16[1024,3,1,384]{3,1,2,0:T(4,128)(2,1)S(1)} async-done(((bf16[1024,3,1,384]{3,1,2,0:T(4,128)(2,1)}), bf16[1024,3,1,384]{3,1,2,0:T(4,128)(2,1)S(1)}, u32[]{:S(2)}, u32[]{:S(2)}) %all-to-all-start.3) | async-done | bytes 2359328 | tf_op jit(solution)/shard_map/all_to_all | solution.py:258
  424.3 333.9 %all-reduce.25.cloned.1.call-done = (bf16[768,2304]{0,1:T(8,128)(2,1)}, bf16[768,768]{1,0:T(8,128)(2,1)}, bf16[768,3072]{1,0:T(8,128)(2,1)}, bf16[3072,768]{1,0:T(8,128)(2,1)}) async-done(((bf16[768,2304]{0,1:T(8,128)(2,1)}, bf16[768,768]{1,0:T(8,128)(2,1)}, bf16[768,3072]{1,0:T(8,128)(2,1)}, bf16[3072,768]{1,0:T(8,128)(2,1)}), (bf16[768,2304]{0,1:T(8,128)(2,1)}, bf16[768,768]{1,0:T(8,128)(2,1)}, ...) | async-done | bytes 14155792 | tf_op jit(solution)/shard_map/psum | solution.py:280
  767.2 7.3 convert_element_type.238
  774.6 6.9 convert_element_type.240
  782.8 40.3 %all-reduce.18 = (f32[1]{0:T(128)}, f32[1]{0:T(128)}, f32[1]{0:T(128)}, f32[]{:T(128)}) all-reduce(f32[1]{0:T(128)} %bitcast.38, f32[1]{0:T(128)} %bitcast.37, f32[1]{0:T(128)} %bitcast.36, f32[]{:T(128)} %get-tuple-element.662), channel_id=1, replica_groups=mesh['seq'=2,'fsdp'=16] {'seq','fsdp'}, use_global_device_ids=true, to_apply=%region_56.57 | all-reduce | flops 4 | bytes 32 | tf_op jit(solution)/shard_map/psum | solution.py:177
  826.6 9.1 all-reduce.21
  835.7 59.7 %all-reduce.19 = (f32[768]{0:T(1024)S(1)}, f32[768]{0:T(1024)S(1)}, f32[768]{0:T(1024)S(1)}, f32[768]{0:T(1024)S(1)}, f32[768]{0:T(1024)S(1)}, /*index=5*/f32[30...) all-reduce(bf16[768]{0:T(1024)(128)(2,1)S(1)} %get-tuple-element.64, ...), channel_id=6, replica_groups=mesh['seq'=2,'fsdp'=16] {'fsdp'}, use_global_device_ids=true, to_apply=%region_26.27.clone | all-reduce | flops 9216 | bytes 55296
  906.4 13.9 %reduce-scatter.13.cloned.1.call-done = f32[48,2304]{1,0:T(8,128)} async-done(((f32[768,2304]{1,0:T(8,128)}), f32[48,2304]{1,0:T(8,128)}) %reduce-scatter.13.cloned.1.call-update) | async-done | bytes 442384
  920.3 115.6 %reduce-scatter.9.cloned.1.call-done = f32[48,3072]{1,0:T(8,128)} async-done(((f32[768,3072]{1,0:T(8,128)}), f32[48,3072]{1,0:T(8,128)}) %reduce-scatter.9.cloned.1.call-update) | async-done | bytes 589840 | tf_op jit(solution)/shard_map/reduce_scatter | solution.py:297
  1035.9 115.5 %reduce-scatter.11.cloned.1.call-done = f32[192,768]{1,0:T(8,128)} async-done(((f32[3072,768]{1,0:T(8,128)}), f32[192,768]{1,0:T(8,128)}) %reduce-scatter.11.cloned.1.call-update) | async-done | bytes 589840 | tf_op jit(solution)/shard_map/reduce_scatter | solution.py:298
  (265 shorter events, 189.5 us)
Async XLA Ops:
  7.2 76.4 %all-gather.5.cloned.1.call-start = ((), (), s32[]{:S(2)}) async-start(), calls=%async_computation.8 | async-start | bytes 3760128 | tf_op jit(solution)/shard_map/all_gather | solution.py:61
  7.9 204.6 %all-gather.7.cloned.1.call-start = ((), (), s32[]{:S(2)}) async-start(), calls=%async_computation.9 | async-start | bytes 1253376 | tf_op jit(solution)/shard_map/all_gather | solution.py:62
  8.7 207.7 %all-gather.9.cloned.1.call-start = ((), (), s32[]{:S(2)}) async-start(), calls=%async_computation.10 | async-start | bytes 5013504 | tf_op jit(solution)/shard_map/all_gather | solution.py:156
  95.7 27.3 %all-to-all-start = ((bf16[512,3,2,384]{3,0,1,2:T(8,128)(2,1)}), bf16[512,3,2,384]{3,0,1,2:T(8,128)(2,1)S(1)}, u32[]{:S(2)}, u32[]{:S(2)}) async-start(bf16[512,3,2,384]{3,0,1,2:T(8,128)(2,1)} %copy.86), calls=%async_computation | async-start | bytes 4718592 | tf_op jit(solution)/shard_map/all_to_all | solution.py:87
  99.6 136.6 %all-gather.11.cloned.1.call-start = ((), (), s32[]{:S(2)}) async-start(), calls=%async_computation.11 | async-start | bytes 5013504 | tf_op jit(solution)/shard_map/all_gather | solution.py:157
  105.4 21.6 %copy-start.19 = (s32[1024]{0:T(1024)}, s32[1024]{0:T(1024)S(1)}, u32[]{:S(2)}) copy-start(s32[1024]{0:T(1024)S(1)} %fusion.50) | copy-start | bytes 12292
  155.7 32.3 %copy-start.17 = (s32[1024]{0:T(1024)S(1)}, s32[1024]{0:T(1024)}, u32[]{:S(2)}) copy-start(s32[1024]{0:T(1024)} %broadcast_clamp_fusion) | copy-start | bytes 12292
  194.7 12.8 %all-to-all-start.1 = ((bf16[2,2,98304]{2,1,0:T(2,128)(2,1)}), bf16[2,2,98304]{2,1,0:T(2,128)(2,1)}, u32[]{:S(2)}, u32[]{:S(2)}) async-start(bf16[2,2,98304]{2,1,0:T(2,128)(2,1)} %reshape.336), calls=%async_computation.1 | async-start | bytes 1572864 | tf_op jit(solution)/shard_map/all_to_all | solution.py:143
  199.5 13.1 %copy-start.8 = (bf16[1,512,768]{2,1,0:T(8,128)(2,1)S(1)}, bf16[1,512,768]{2,1,0:T(8,128)(2,1)}, u32[]{:S(2)}) copy-start(bf16[1,512,768]{2,1,0:T(8,128)(2,1)} %param.22) | copy-start | bytes 2359300
  200.2 59.8 %copy-start.23 = (f32[768]{0:T(1024)}, f32[768]{0:T(1024)S(1)}, u32[]{:S(2)}) copy-start(f32[768]{0:T(1024)S(1)} %convert_element_type.214) | copy-start | bytes 9220
  200.2 36.0 %copy-start.37 = (f32[768]{0:T(1024)}, f32[768]{0:T(1024)S(1)}, u32[]{:S(2)}) copy-start(f32[768]{0:T(1024)S(1)} %convert_element_type.215) | copy-start | bytes 9220
  216.0 44.0 %copy-start.4 = (f32[512,768]{1,0:T(8,128)}, f32[512,768]{1,0:T(8,128)S(1)}, u32[]{:S(2)}) copy-start(f32[512,768]{1,0:T(8,128)S(1)} %get-tuple-element.679) | copy-start | bytes 4718596
  216.0 44.0 %copy-start.21 = (f32[512]{0:T(512)}, f32[512]{0:T(512)S(1)}, u32[]{:S(2)}) copy-start(f32[512]{0:T(512)S(1)} %broadcast_multiply_fusion.1) | copy-start | bytes 6148
  216.3 43.7 %copy-start.29 = (f32[512]{0:T(512)}, f32[512]{0:T(512)S(1)}, u32[]{:S(2)}) copy-start(f32[512]{0:T(512)S(1)} %fusion.53) | copy-start | bytes 6148
  245.2 11.1 slice-start
  261.7 13.3 %copy-start.20 = (s32[1024]{0:T(1024)S(1)}, s32[1024]{0:T(1024)}, u32[]{:S(2)}) copy-start(s32[1024]{0:T(1024)} %copy-done.19) | copy-start | bytes 12292
  263.5 11.5 all-to-all-start.2
  326.3 9.5 copy-start.2
  383.2 32.6 %all-to-all-start.3 = ((bf16[1024,3,1,384]{3,1,2,0:T(4,128)(2,1)}), bf16[1024,3,1,384]{3,1,2,0:T(4,128)(2,1)S(1)}, u32[]{:S(2)}, u32[]{:S(2)}) async-start(bf16[1024,3,1,384]{3,1,2,0:T(4,128)(2,1)} %bitcast.149), calls=%async_computation.3 | async-start | bytes 6291456 | tf_op jit(solution)/shard_map/all_to_all | solution.py:258
  387.2 371.0 %all-reduce.25.cloned.1.call-start = ((), (), s32[]{:S(2)}) async-start(), calls=%async_computation.16 | async-start | bytes 28311552 | tf_op jit(solution)/shard_map/psum | solution.py:280
  424.3 482.2 %reduce-scatter.7.cloned.1.call-start = ((), (), s32[]{:S(2)}) async-start(), calls=%async_computation.12 | async-start | bytes 2506752 | tf_op jit(solution)/shard_map/reduce_scatter | solution.py:296
  761.1 159.2 %reduce-scatter.13.cloned.1.call-start = ((), (), s32[]{:S(2)}) async-start(), calls=%async_computation.15 | async-start | bytes 7520256
  767.1 268.8 %reduce-scatter.9.cloned.1.call-start = ((), (), s32[]{:S(2)}) async-start(), calls=%async_computation.13 | async-start | bytes 10027008 | tf_op jit(solution)/shard_map/reduce_scatter | solution.py:297
  774.5 376.9 %reduce-scatter.11.cloned.1.call-start = ((), (), s32[]{:S(2)}) async-start(), calls=%async_computation.14 | async-start | bytes 10027008 | tf_op jit(solution)/shard_map/reduce_scatter | solution.py:298
  781.4 45.1 %copy-start.31 = (bf16[768]{0:T(1024)(128)(2,1)S(1)}, bf16[768]{0:T(1024)(128)(2,1)}, u32[]{:S(2)}) copy-start(bf16[768]{0:T(1024)(128)(2,1)} %get-tuple-element.580) | copy-start | bytes 4612
  781.4 45.1 %copy-start.32 = (bf16[768]{0:T(1024)(128)(2,1)S(1)}, bf16[768]{0:T(1024)(128)(2,1)}, u32[]{:S(2)}) copy-start(bf16[768]{0:T(1024)(128)(2,1)} %get-tuple-element.582) | copy-start | bytes 4612
  781.4 45.1 %copy-start.33 = (bf16[768]{0:T(1024)(128)(2,1)S(1)}, bf16[768]{0:T(1024)(128)(2,1)}, u32[]{:S(2)}) copy-start(bf16[768]{0:T(1024)(128)(2,1)} %get-tuple-element.664) | copy-start | bytes 4612
  781.5 45.1 %copy-start.34 = (bf16[768]{0:T(1024)(128)(2,1)S(1)}, bf16[768]{0:T(1024)(128)(2,1)}, u32[]{:S(2)}) copy-start(bf16[768]{0:T(1024)(128)(2,1)} %get-tuple-element.668) | copy-start | bytes 4612
  781.5 45.1 %copy-start.35 = (bf16[3072]{0:T(1024)(128)(2,1)S(1)}, bf16[3072]{0:T(1024)(128)(2,1)}, u32[]{:S(2)}) copy-start(bf16[3072]{0:T(1024)(128)(2,1)} %get-tuple-element.666) | copy-start | bytes 18436
  781.5 45.1 %copy-start.45 = (bf16[768]{0:T(1024)(128)(2,1)S(1)}, bf16[768]{0:T(1024)(128)(2,1)}, u32[]{:S(2)}) copy-start(bf16[768]{0:T(1024)(128)(2,1)} %get-tuple-element.569) | copy-start | bytes 4612
  781.5 45.1 %copy-start.46 = (bf16[768]{0:T(1024)(128)(2,1)S(1)}, bf16[768]{0:T(1024)(128)(2,1)}, u32[]{:S(2)}) copy-start(bf16[768]{0:T(1024)(128)(2,1)} %get-tuple-element.575) | copy-start | bytes 4612
  781.5 119.2 %copy-start.28 = (f32[512]{0:T(512)S(1)}, f32[512]{0:T(512)}, u32[]{:S(2)}) copy-start(f32[512]{0:T(512)} %copy-done.27) | copy-start | bytes 6148
  (37 other events, 223.3 us)
Sparse Core Ops, SparseCore 0:
  10.3 50.2 all-gather.4
  62.8 36.8 all-gather.6
  102.0 51.9 all-gather.8
  156.1 51.7 all-gather.10
  424.4 333.7 all-reduce.24
  762.4 63.8 reduce-scatter.6
  830.9 89.4 reduce-scatter.12
  925.0 110.9 reduce-scatter.8
  1040.6 110.8 reduce-scatter.10
where the time goes:
time: 1170 us; the launch traced here: 1160 us
  waiting for transfers between devices  627 us (54%)
  blocking collectives  173 us (15%)
  matrix products  142 us (12%)
  local copies, waits for them, and re-layouts  115 us (10%)
  other arithmetic  66 us (6%)
  between operations  19 us (2%)
  starting transfers between devices  16.5 us (1%)
    psum x1, waiting for transfers between devices, body(): lax.psum(grad_w_qkv.astype(jnp.bfloat16), 'seq').astype(jnp.float32)  334 us
    unnamed x2, blocking collectives  124 us
    reduce_scatter x1, waiting for transfers between devices, body(): lax.psum_scatter(pair_in, 'fsdp', scatter_dimension=0, tiled=True)  116 us
    reduce_scatter x1, waiting for transfers between devices, body(): lax.psum_scatter(pair_back, 'fsdp', scatter_dimension=0, tiled=True)  116 us
    psum x1, blocking collectives, body(): lax.psum((jnp.sum(valid_rows * tokens_f * tokens_f), jnp.sum(valid_rows *...  40.3 us
    dot_general x4, matrix products, block_scores(): jnp.einsum('qhd,khd->hqk', query_blk, key_pos, preferred_element_type=jnp...  33.6 us
    unnamed x132, local copies, waits for them, and re-layouts  24.9 us
  transfers between devices with their start and end apart: 13, of which 8 were waited for; matrix products, arithmetic and copies ran while one was open for 15% of the time, Pallas kernels for 0%

commit v1 on v0

v1 whole, which is shorter than its diff:
```python
import math

import jax
import jax.numpy as jnp
from jax import lax
from jax.sharding import PartitionSpec as P

HD = 64
eps_norm = 1e-05
masked_fill = -1e30
f32 = jnp.float32
bf16 = jnp.bfloat16


def layer_norm(values, gain, shift):
    average = jnp.mean(values, axis=-1, keepdims=True)
    centered = values - average
    variance = jnp.mean(centered * centered, axis=-1, keepdims=True)
    return centered * lax.rsqrt(variance + eps_norm) * gain + shift


def gelu_exact(values):
    return jax.nn.gelu(values, approximate=False)


def contract_rows(left, right):
    return lax.dot_general(left, right, (((0,), (0,)), ((), ())), preferred_element_type=f32)


def contract_cols(left, right):
    return lax.dot_general(left, right, (((1,), (1,)), ((), ())), preferred_element_type=f32)


def bits_of(count):
    return [1 << k for k in range(count.bit_length() - 1)]


def swap(value, axis, bit):
    count = lax.axis_size(axis)
    return lax.ppermute(value, axis, [(i, i ^ bit) for i in range(count)])


def gather_blocks(shard, axis):
    me = lax.axis_index(axis)
    held = shard[None]
    for bit in reversed(bits_of(lax.axis_size(axis))):
        other = swap(held, axis, bit)
        high = (me & bit) != 0
        first = jnp.where(high, other, held)
        second = jnp.where(high, held, other)
        held = jnp.stack([first, second], axis=1).reshape((-1,) + shard.shape)
    return held


def reduce_blocks(part, over_seq, wire):
    me = lax.axis_index("fsdp")
    side = lax.axis_index("seq")
    keep = part
    width = part.shape[2]
    for bit in bits_of(lax.axis_size("fsdp")):
        pairs = keep.reshape((keep.shape[0] // 2, 2) + keep.shape[1:])
        mine = ((me & bit) != 0).astype(jnp.int32)
        sent = lax.dynamic_index_in_dim(pairs, 1 - mine, 1, keepdims=False).astype(wire)
        kept = lax.dynamic_index_in_dim(pairs, mine, 1, keepdims=False)
        keep = (kept.astype(f32) + swap(sent, "fsdp", bit).astype(f32)).astype(wire)
        if over_seq and bit == 1:
            half = width // 2
            sent = lax.dynamic_slice_in_dim(keep, (1 - side) * half, half, 2)
            kept = lax.dynamic_slice_in_dim(keep, side * half, half, 2)
            keep = (kept.astype(f32) + swap(sent, "seq", 1).astype(f32)).astype(wire)
    own = keep[0]
    if not over_seq:
        return own
    other = swap(own, "seq", 1)
    return jnp.where(
        side == 0, jnp.concatenate([own, other], 1), jnp.concatenate([other, own], 1)
    )


def body(
    tokens, prior_logits, lengths, order, cotangent, w_qkv, w_out, w_in, w_back,
    bias_q, bias_v, bias_o, gain_one, shift_one, bias_in, bias_back, gain_two, shift_two,
):
    side = lax.axis_index("seq")
    me = lax.axis_index("fsdp")
    groups = lax.axis_size("fsdp")
    rows = tokens[0]
    local_count, width = rows.shape
    total = 2 * local_count
    heads_local = prior_logits.shape[1]
    local_width = heads_local * HD
    scale = 1.0 / math.sqrt(HD)
    piece = bias_q.shape[0]

    other_rows = swap(rows, "seq", 1)
    own_qkv = lax.dynamic_index_in_dim(
        w_qkv.reshape(w_qkv.shape[0], 3, 2, local_width), side, 2, keepdims=False
    ).reshape(w_qkv.shape[0], 3 * local_width)
    small = jnp.concatenate(
        [bias_q, bias_v, bias_o, gain_one, shift_one, bias_back, gain_two, shift_two, bias_in]
    )[None]
    small_all = gather_blocks(small, "fsdp")[:, 0]
    query_bias, value_bias, proj_bias, first_gain, first_shift, outer_bias, second_gain, second_shift = (
        small_all[:, k * piece : (k + 1) * piece].reshape(width).astype(f32) for k in range(8)
    )
    inner_bias = small_all[:, 8 * piece :].reshape(-1).astype(f32)
    qkv_weight = gather_blocks(own_qkv, "fsdp").reshape(width, 3 * local_width)
    proj_weight = gather_blocks(w_out, "fsdp").reshape(width, width)
    inner_weight = gather_blocks(w_in, "fsdp").reshape(width, -1)
    outer_weight = gather_blocks(w_back, "fsdp").reshape(-1, width)

    order_row = order[0]
    length = lengths[0]
    own_order = lax.dynamic_slice_in_dim(order_row, side * local_count, local_count)
    other_order = lax.dynamic_slice_in_dim(order_row, (1 - side) * local_count, local_count)
    positions = jnp.arange(total, dtype=jnp.int32)
    own_pick = (positions[:, None] == own_order[None, :]).astype(bf16)
    other_pick = (positions[:, None] == other_order[None, :]).astype(bf16)

    def to_positions(own, other):
        return (
            jnp.dot(own_pick, own, preferred_element_type=f32)
            + jnp.dot(other_pick, other, preferred_element_type=f32)
        ).astype(bf16)

    placed_rows = to_positions(rows, other_rows)
    own_cols = lambda vector: lax.dynamic_slice_in_dim(vector, side * local_width, local_width)
    joint_bias = jnp.concatenate(
        [own_cols(query_bias), jnp.zeros((local_width,), f32), own_cols(value_bias)]
    )
    joint = (jnp.dot(placed_rows, qkv_weight, preferred_element_type=f32) + joint_bias).astype(bf16)
    placed = joint.reshape(total, 3, local_width)
    query_pos = placed[:, 0].reshape(total, heads_local, HD)
    key_pos = placed[:, 1].reshape(total, heads_local, HD)
    value_pos = placed[:, 2].reshape(total, heads_local, HD)
    key_valid = (positions < length)[None, None, :]
    prior = prior_logits[0]
    block = min(512, total)
    block_count = total // block

    def block_scores(start):
        query_blk = lax.dynamic_slice_in_dim(query_pos, start, block, 0)
        prior_blk = lax.dynamic_slice_in_dim(prior, start, block, 1).astype(f32)
        scores = (
            jnp.einsum("qhd,khd->hqk", query_blk, key_pos, preferred_element_type=f32) * scale
            + prior_blk
        )
        return (query_blk, scores)

    def forward_block(block_index, carry):
        raw_buf, context_buf, lse_buf = carry
        start = block_index * block
        query_blk, scores = block_scores(start)
        masked = jnp.where(key_valid, scores, masked_fill)
        largest = jnp.max(masked, axis=-1, keepdims=True)
        exponent = jnp.exp(masked - largest)
        row_total = jnp.sum(exponent, axis=-1, keepdims=True)
        weights = (exponent / row_total).astype(bf16)
        context_blk = jnp.einsum(
            "hqk,khd->qhd", weights, value_pos, preferred_element_type=f32
        ).astype(bf16)
        raw_buf = lax.dynamic_update_slice_in_dim(raw_buf, scores.astype(bf16), start, 1)
        context_buf = lax.dynamic_update_slice_in_dim(context_buf, context_blk, start, 0)
        lse_buf = lax.dynamic_update_slice_in_dim(lse_buf, largest + jnp.log(row_total), start, 1)
        return (raw_buf, context_buf, lse_buf)

    raw_buf, context_pos, lse_buf = lax.fori_loop(
        0,
        block_count,
        forward_block,
        (
            jnp.zeros((heads_local, total, total), bf16),
            jnp.zeros((total, heads_local, HD), bf16),
            jnp.zeros((heads_local, total, 1), f32),
        ),
    )
    context_pos = context_pos.reshape(total, local_width)
    context_sent = contract_rows(other_pick, context_pos).astype(bf16)
    context_own = contract_rows(own_pick, context_pos).astype(bf16)
    context_got = swap(context_sent, "seq", 1)
    context = jnp.where(
        side == 0,
        jnp.concatenate([context_own, context_got], 1),
        jnp.concatenate([context_got, context_own], 1),
    )
    attended = jnp.dot(context, proj_weight, preferred_element_type=f32) + proj_bias
    tokens_f = rows.astype(f32)
    residual_one = tokens_f + attended
    hidden, norm_back_one = jax.vjp(layer_norm, residual_one, first_gain, first_shift)
    hidden_low = hidden.astype(bf16)
    inner = jnp.dot(hidden_low, inner_weight, preferred_element_type=f32) + inner_bias
    activated_f, gelu_back = jax.vjp(gelu_exact, inner)
    activated = activated_f.astype(bf16)
    branch = jnp.dot(activated, outer_weight, preferred_element_type=f32) + outer_bias
    residual_two = hidden + branch
    normed_two, norm_back_two = jax.vjp(layer_norm, residual_two, second_gain, second_shift)
    valid_rows = (own_order < length).astype(f32)[:, None]
    stats = jnp.stack(
        [
            jnp.sum(valid_rows * tokens_f * tokens_f),
            jnp.sum(valid_rows * attended * attended),
            jnp.sum(valid_rows * branch * branch),
            jnp.sum(valid_rows),
        ]
    )
    d_output = cotangent[0].astype(f32) * valid_rows
    d_res_two, grad_gain_two, grad_shift_two = norm_back_two(d_output)
    d_branch = d_res_two.astype(bf16)
    grad_bias_back = jnp.sum(d_branch.astype(f32), axis=0)
    grad_w_back = contract_rows(activated, d_branch).astype(bf16)
    d_activated = contract_cols(d_branch, outer_weight)
    d_inner = gelu_back(d_activated)[0].astype(bf16)
    grad_bias_in = jnp.sum(d_inner.astype(f32), axis=0)
    grad_w_in = contract_rows(hidden_low, d_inner).astype(bf16)
    d_hidden = d_res_two + contract_cols(d_inner, inner_weight)
    d_res_one, grad_gain_one, grad_shift_one = norm_back_one(d_hidden)
    d_attended = d_res_one.astype(bf16)
    grad_bias_o = jnp.sum(d_attended.astype(f32), axis=0)
    grad_w_out = contract_rows(context, d_attended).astype(bf16)
    d_context = contract_cols(d_attended, proj_weight).astype(bf16)
    d_context_own = lax.dynamic_slice_in_dim(d_context, side * local_width, local_width, 1)
    d_context_sent = lax.dynamic_slice_in_dim(d_context, (1 - side) * local_width, local_width, 1)
    d_context_pos = to_positions(d_context_own, swap(d_context_sent, "seq", 1)).reshape(
        total, heads_local, HD
    )

    out_back = reduce_blocks(grad_w_back.reshape(groups, -1, width), True, bf16)
    out_in = reduce_blocks(grad_w_in.reshape(groups, piece, -1), True, bf16)
    out_out = reduce_blocks(grad_w_out.reshape(groups, piece, width), True, bf16)
    by_owner = lambda vector: vector.reshape(groups, -1)
    vectors = jnp.concatenate(
        [by_owner(v) for v in (grad_bias_o, grad_gain_one, grad_shift_one, grad_bias_back,
                               grad_gain_two, grad_shift_two, grad_bias_in)]
        + [jnp.broadcast_to(stats[None], (groups, 4))],
        axis=1,
    )
    vectors = reduce_blocks(vectors[:, None], False, f32)
    vectors = (vectors + swap(vectors, "seq", 1))[0]
    stats = vectors[10 * piece :]
    rms = jnp.sqrt(stats[:3] / (stats[3] * width))

    def backward_block(block_index, carry):
        dprior_buf, dquery_buf, dkey_acc, dvalue_acc = carry
        start = block_index * block
        query_blk, scores = block_scores(start)
        masked = jnp.where(key_valid, scores, masked_fill)
        lse_blk = lax.dynamic_slice_in_dim(lse_buf, start, block, 1)
        probability = jnp.exp(masked - lse_blk)
        weights = probability.astype(bf16)
        dcontext_blk = lax.dynamic_slice_in_dim(d_context_pos, start, block, 0)
        d_prob = jnp.einsum("qhd,khd->hqk", dcontext_blk, value_pos, preferred_element_type=f32)
        row_term = jnp.sum(probability * d_prob, axis=-1, keepdims=True)
        d_scores = (probability * (d_prob - row_term)).astype(bf16)
        dprior_buf = lax.dynamic_update_slice_in_dim(dprior_buf, d_scores, start, 1)
        dquery_blk = (
            jnp.einsum("hqk,khd->qhd", d_scores, key_pos, preferred_element_type=f32) * scale
        )
        dquery_buf = lax.dynamic_update_slice_in_dim(dquery_buf, dquery_blk, start, 0)
        dkey_acc = (
            dkey_acc
            + jnp.einsum("hqk,qhd->khd", d_scores, query_blk, preferred_element_type=f32) * scale
        )
        dvalue_acc = dvalue_acc + jnp.einsum(
            "hqk,qhd->khd", weights, dcontext_blk, preferred_element_type=f32
        )
        return (dprior_buf, dquery_buf, dkey_acc, dvalue_acc)

    dprior_buf, dquery_buf, dkey_acc, dvalue_acc = lax.fori_loop(
        0,
        block_count,
        backward_block,
        (
            jnp.zeros((heads_local, total, total), bf16),
            jnp.zeros((total, heads_local, HD), f32),
            jnp.zeros((total, heads_local, HD), f32),
            jnp.zeros((total, heads_local, HD), f32),
        ),
    )
    d_joint = jnp.concatenate(
        [
            dquery_buf.reshape(total, local_width),
            dkey_acc.reshape(total, local_width),
            dvalue_acc.reshape(total, local_width),
        ],
        axis=1,
    ).astype(bf16)
    grad_w_qkv = contract_rows(placed_rows, d_joint).astype(bf16)
    d_rows = contract_cols(d_joint, qkv_weight).astype(bf16)
    d_rows_sent = contract_rows(other_pick, d_rows).astype(bf16)
    d_rows_own = contract_rows(own_pick, d_rows)
    tokens_grad = (d_res_one + d_rows_own + swap(d_rows_sent, "seq", 1).astype(f32)).astype(bf16)
    bias_sums = jnp.sum(d_joint.astype(f32), axis=0)
    spread = lambda vector: lax.dynamic_update_slice(
        jnp.zeros((width,), f32), vector, (side * local_width,)
    ).reshape(groups, piece)
    late = jnp.concatenate(
        [spread(bias_sums[:local_width]), spread(bias_sums[2 * local_width :])], axis=1
    )
    late = reduce_blocks(late[:, None], False, f32)
    late = (late + swap(late, "seq", 1))[0]
    own_part = reduce_blocks(grad_w_qkv.reshape(groups, piece, -1), False, bf16)
    other_part = swap(own_part, "seq", 1)
    first = jnp.where(side == 0, own_part, other_part).reshape(piece, 3, 1, local_width)
    second = jnp.where(side == 0, other_part, own_part).reshape(piece, 3, 1, local_width)
    out_qkv = jnp.concatenate([first, second], axis=2).reshape(piece, 3 * width)
    take = lambda k: vectors[k * piece : (k + 1) * piece]
    return (
        normed_two.astype(bf16)[None],
        raw_buf[None],
        tokens_grad[None],
        dprior_buf[None],
        out_qkv.astype(f32),
        out_out.astype(f32),
        out_in.astype(f32),
        out_back.astype(f32),
        late[:piece],
        late[piece:],
        take(0),
        take(1),
        take(2),
        vectors[6 * piece : 10 * piece],
        take(3),
        take(4),
        take(5),
        rms,
    )


def solution(mesh):
    shard = P("fsdp", "seq", None)
    heads = P("fsdp", "seq", None, None)
    mat = P("fsdp", None)
    vec = P("fsdp")
    return jax.shard_map(
        body,
        mesh=mesh,
        in_specs=(shard, heads, vec, mat, shard) + (mat,) * 4 + (vec,) * 9,
        out_specs=(shard, heads, shard, heads) + (mat,) * 4 + (vec,) * 9 + (P(),),
        check_vma=False,
    )
```

time: 1170 us -> 508 us (0.43)
  waiting for transfers between devices: 627 us -> 158 us
  blocking collectives: 173 us -> 0 us
  local copies, waits for them, and re-layouts: 115 us -> 55.6 us
  starting transfers between devices: 16.5 us -> 65.3 us
  between operations: 19 us -> 3.78 us
    psum x1 -> x0, waiting for transfers between devices: 334 us -> none  [body(): lax.psum(grad_w_qkv.astype(jnp.bfloat16), 'seq').astype(jnp.float32)]
    reduce_scatter x3 -> x0, waiting for transfers between devices: 231 us -> none  [the longest x1 116 us: body(): lax.psum_scatter(pair_in, 'fsdp', scatter_dimension=0, tiled=True)]
    ppermute x0 -> x57, waiting for transfers between devices: none -> 158 us  [swap(): return lax.ppermute(value, axis, [(i, i ^ bit) for i in range(count)])]
    unnamed x2 -> x0, blocking collectives: 124 us -> none
    ppermute x0 -> x57, starting transfers between devices: none -> 65.3 us  [swap(): return lax.ppermute(value, axis, [(i, i ^ bit) for i in range(count)])]
    psum x2 -> x0, blocking collectives: 49.3 us -> none  [the longest x1 40.3 us: body(): lax.psum((jnp.sum(valid_rows * tokens_f * tokens_f), jnp.sum(valid_rows *...]
    all_to_all x4 -> x0, waiting for transfers between devices: 45.5 us -> none  [the longest x1 17.6 us: body(): lax.all_to_all(joint, 'seq', split_axis=2, concat_axis=0, tiled=True)]
    gather x5 -> x0, local copies, waits for them, and re-layouts: 28.5 us -> none  [the longest x1 10.2 us: body(): d_joint_stored = d_joint_pos[order_row].reshape(total, 3, 1, local_width)]
  transfers between devices with their start and end apart: 13 -> 57, of which waited for: 8 -> 30; matrix products, arithmetic and copies ran while one was open for 15% -> 38% of each run, Pallas kernels for 0% -> 0%
where the time goes in v1:
time: 508 us; the launch traced here: 500 us
  waiting for transfers between devices  158 us (31%)
  matrix products  143 us (28%)
  other arithmetic  73.4 us (14%)
  starting transfers between devices  65.3 us (13%)
  local copies, waits for them, and re-layouts  55.6 us (11%)
    ppermute x57, waiting for transfers between devices, swap(): return lax.ppermute(value, axis, [(i, i ^ bit) for i in range(count)])  158 us
    ppermute x57, starting transfers between devices, swap(): return lax.ppermute(value, axis, [(i, i ^ bit) for i in range(count)])  65.3 us
    dot_general x4, matrix products, block_scores(): jnp.einsum('qhd,khd->hqk', query_blk, key_pos, preferred_element_type=f32)  33.8 us
    dot_general x4, matrix products, contract_cols(): lax.dot_general(left, right, (((1,), (1,)), ((), ())), preferred_element_...  20.3 us
    dot_general x8, matrix products, contract_rows(): lax.dot_general(left, right, (((0,), (0,)), ((), ())), preferred_element_...  20.2 us
    dot_general x1, matrix products, body(): jnp.dot(hidden_low, inner_weight, preferred_element_type=f32) + inner_bias  18.5 us
    dynamic_update_slice x2, other arithmetic, backward_block(): dprior_buf = lax.dynamic_update_slice_in_dim(dprior_buf, d_scores, start, 1)  17.9 us
    dot_general x2, matrix products, backward_block(): jnp.einsum('hqk,qhd->khd', weights, dcontext_blk, preferred_element_type=...  14.4 us
  transfers between devices with their start and end apart: 57, of which 30 were waited for; matrix products, arithmetic and copies ran while one was open for 38% of the time, Pallas kernels for 0%

profile of v1, /device:TPU:0, one launch (start us, length us, event | category | flops | bytes accessed | tf_op | source)
XLA Modules:
  0.0 500.0 jit_solution(16686096070825602285)
XLA Ops:
  0.7 6.1 %concatenate.63 = bf16[576]{0:T(1024)(128)(2,1)S(1)} concatenate(bf16[48]{0:T(256)(128)(2,1)} %param.31, bf16[48]{0:T(256)(128)(2,1)} %param.32, bf16[48]{0:T(256)(128)(2,1)} %param.33, bf16[48]{0:T(256)(128)(2,1)} %param.34, bf16[48]{0:T(256)(128)(2,1)} %param.35, bf16[48]{0:T(256)(128)(2,1)} %param.37, bf16[48]{0:T(256)(128)(2,1)} %param.38, bf16[48]{0:T(256)(128)(2,1)} %param.39, ...), dimensions={0} | concatenate | bytes 2304 | tf_op jit(solution)/shard_map/concatenate | solution.py:99
  6.8 4.1 collective-permute-start.5
  44.7 6.1 %collective-permute-done.11 = bf16[2,48,768]{2,1,0:T(8,128)(2,1)S(1)} collective-permute-done((bf16[2,48,768]{2,1,0:T(8,128)(2,1)S(1)}, bf16[2,48,768]{2,1,0:T(8,128)(2,1)S(1)}, u32[]{:S(2)}, u32[]{:S(2)}) %collective-permute-start.11) | collective-permute-done | bytes 147488 | tf_op jit(solution)/shard_map/ppermute | solution.py:40
  61.1 8.3 %collective-permute-done.3 = bf16[4,48,1152]{2,1,0:T(8,128)(2,1)S(1)} collective-permute-done((bf16[4,48,1152]{2,1,0:T(8,128)(2,1)S(1)}, bf16[4,48,1152]{2,1,0:T(8,128)(2,1)S(1)}, u32[]{:S(2)}, u32[]{:S(2)}) %collective-permute-start.3) | collective-permute-done | bytes 442400 | tf_op jit(solution)/shard_map/ppermute | solution.py:40
  72.0 8.7 %collective-permute-done.15 = bf16[2,48,3072]{2,1,0:T(8,128)(2,1)S(1)} collective-permute-done((bf16[2,48,3072]{2,1,0:T(8,128)(2,1)S(1)}, bf16[2,48,3072]{2,1,0:T(8,128)(2,1)S(1)}, u32[]{:S(2)}, u32[]{:S(2)}) %collective-permute-start.15) | collective-permute-done | bytes 589856 | tf_op jit(solution)/shard_map/ppermute | solution.py:40
  90.8 4.4 copy.114
  97.0 12.9 %collective-permute-done.16 = bf16[4,48,3072]{2,1,0:T(8,128)(2,1)} collective-permute-done((bf16[4,48,3072]{2,1,0:T(8,128)(2,1)S(1)}, bf16[4,48,3072]{2,1,0:T(8,128)(2,1)}, u32[]{:S(2)}, u32[]{:S(2)}) %collective-permute-start.16) | collective-permute-done | bytes 1179680 | tf_op jit(solution)/shard_map/ppermute | solution.py:40
  113.2 20.8 %collective-permute-done.20 = bf16[4,192,768]{2,1,0:T(8,128)(2,1)} collective-permute-done((bf16[4,192,768]{2,1,0:T(8,128)(2,1)}, bf16[4,192,768]{2,1,0:T(8,128)(2,1)}, u32[]{:S(2)}, u32[]{:S(2)}) %collective-permute-start.20) | collective-permute-done | bytes 1179680 | tf_op jit(solution)/shard_map/ppermute | solution.py:40
  138.3 6.4 %broadcast.151.clone = bf16[6,1024,1024]{2,1,0:T(8,128)(2,1)} broadcast(bf16[]{:T(256)} %constant.327.clone.1), dimensions={} | broadcast | bytes 12582914 | tf_op jit(solution)/shard_map/broadcast.24
  144.7 31.3 %while.38 = (s32[]{:T(128)}, bf16[6,1024,1024]{2,1,0:T(8,128)(2,1)}, bf16[1024,6,64]{0,2,1:T(8,128)(2,1)S(1)}, f32[6,1024,1]{1,0,2:T(8,128)S(1)}, bf16[1024,6,64...) while((s32[]{:T(128)}, ...), condition=%wide.region_3.4_spmd.clone, body=%wide.region_0.3_spmd.clone.sunk | while | flops 846395392 | bytes 65397944 | solution.py:167
  145.3 7.3 %convert_dynamic-update-slice_fusion.2 = (bf16[6,1024,1024]{2,1,0:T(8,128)(2,1)}, f32[6,512,1024]{2,1,0:T(8,128)S(1)}) fusion(bf16[6,1024,1024]{2,1,0:T(8,128)(2,1)} %get-tuple-element.748, s32[]{:T(128)S(6)} %select_n.674, bf16[6,1024,1024]{2,1,0:T(8,128)(2,1)} %get-tuple-element.766, bf16[1024,6,64]{0,2,1:T(8,128)(2,1)S(1)} %get-tuple-element.765, ...), kind=kOutput, calls=%fused_computation.7.clone.1 | convolution fusion | flops 415236096 | bytes 26346496 | tf_op jit(solution)/shard_map/while/body/eval_jaxpr/qhd,khd->hqk/dot_general | solution.py:145
  160.9 7.3 %convert_dynamic-update-slice_fusion.2 = (bf16[6,1024,1024]{2,1,0:T(8,128)(2,1)}, f32[6,512,1024]{2,1,0:T(8,128)S(1)}) fusion(bf16[6,1024,1024]{2,1,0:T(8,128)(2,1)} %get-tuple-element.748, s32[]{:T(128)S(6)} %select_n.674, bf16[6,1024,1024]{2,1,0:T(8,128)(2,1)} %get-tuple-element.766, bf16[1024,6,64]{0,2,1:T(8,128)(2,1)S(1)} %get-tuple-element.765, ...), kind=kOutput, calls=%fused_computation.7.clone.1 | convolution fusion | flops 415236096 | bytes 26346496 | tf_op jit(solution)/shard_map/while/body/eval_jaxpr/qhd,khd->hqk/dot_general | solution.py:145
  179.5 8.2 %collective-permute-done.9 = bf16[512,384]{0,1:T(8,128)(2,1)S(1)} collective-permute-done((bf16[512,384]{0,1:T(8,128)(2,1)S(1)}, bf16[512,384]{0,1:T(8,128)(2,1)S(1)}, u32[]{:S(2)}, u32[]{:S(2)}) %collective-permute-start.9) | collective-permute-done | bytes 393248 | tf_op jit(solution)/shard_map/ppermute | solution.py:40
  196.4 18.5 %multiply_convert_fusion.1 = (bf16[512,3072]{1,0:T(8,128)(2,1)S(1)}, f32[512,3072]{1,0:T(8,128)}, f32[512,3072]{1,0:T(8,128)}) fusion(f32[3072]{0:T(1024)S(1)} %copy-done.31, bf16[768,3072]{1,0:T(8,128)(2,1)S(1)} %bitcast.433, f32[512,768]{1,0:T(8,128)S(1)} %get-tuple-element.519, f32[768]{0:T(1024)S(1)} %copy-done.37, f32[768]{0:T(1024)S(1)} %copy-done.28, ...), kind=kOutput, calls=%fused_computation.43 | convolution fusion | flops 2521694208 | bytes 22042624 | tf_op jit(solution)/shard_map/dot_general | solution.py:191
  222.4 8.9 %convert_reduce_fusion = (f32[3072]{0:T(1024)S(1)}, bf16[512,3072]{1,0:T(8,128)(2,1)}) fusion(f32[512,3072]{1,0:T(8,128)} %get-tuple-element.517, f32[512,3072]{1,0:T(8,128)} %get-tuple-element.591, f32[3072]{0:T(1024)S(1)} %copy-done.31, bf16[512,768]{1,0:T(8,128)(2,1)S(1)} %get-tuple-element.507, bf16[3072,768]{1,0:T(8,128)(2,1)S(1)} %bitcast.432), kind=kOutput, calls=%fused_computation.41 | convolution fusion | flops 2442654720 | bytes 21258240 | tf_op jit(solution)/shard_map/dot_general | solution.py:31
  231.3 6.3 %multiply_reduce_fusion.1 = (f32[768]{0:T(1024)S(1)}, f32[512]{0:T(512)S(1)}, f32[768]{0:T(1024)S(1)}, f32[512,768]{1,0:T(8,128)}) fusion(f32[512,768]{1,0:T(8,128)S(1)} %get-tuple-element.519, f32[512]{0:T(512)S(1)} %fusion.101, f32[512]{0:T(512)S(1)} %broadcast_multiply_fusion.1, f32[768]{0:T(1024)S(1)} %copy-done.28, ...), kind=kOutput, calls=%fused_computation.112 | convolution fusion | flops 2419849216 | bytes 12600320 | tf_op jit(solution)/shard_map/dot_general | solution.py:31
  237.6 4.8 convolution_convert_fusion.1
  242.4 4.8 convolution_convert_fusion
  287.2 6.4 %broadcast.151 = bf16[6,1024,1024]{2,1,0:T(8,128)(2,1)} broadcast(bf16[]{:T(256)} %constant.327.clone.1), dimensions={} | broadcast | bytes 12582914 | tf_op jit(solution)/shard_map/broadcast.24
  293.6 66.2 %while.39 = (s32[]{:T(128)}, bf16[6,1024,1024]{2,1,0:T(8,128)(2,1)}, bf16[1024,6,64]{0,2,1:T(8,128)(2,1)}, f32[1024,6,64]{0,2,1:T(8,128)S(1)}, f32[1024,6,64]{0,...) while((s32[]{:T(128)}, ...), condition=%wide.region_14.15_spmd.clone, body=%wide.region_12.14_spmd.clone.sunk | while | flops 2050029568 | bytes 127470920 | solution.py:268
  297.6 9.5 %multiply_reduce_fusion.6 = (f32[6,512]{1,0:T(8,128)S(1)}, f32[6,512,1024]{2,1,0:T(8,128)}) fusion(f32[6,512,1024]{2,1,0:T(8,128)S(1)} %fusion.181, f32[6,512]{1,0:T(8,128)S(1)} %dynamic-slice_bitcast_fusion.15, bf16[6,1024,1024]{2,1,0:T(8,128)(2,1)} %get-tuple-element.812, s32[]{:T(128)S(6)} %select_n.675, ...), kind=kOutput, calls=%fused_computation.18.clone.1 | convolution fusion | flops 424670208 | bytes 32667648 | tf_op jit(solution)/shard_map/while/body/eval_jaxpr/qhd,khd->hqk/dot_general | solution.py:145
  307.1 7.0 %bitcast_add_fusion.6 = f32[1024,6,64]{0,2,1:T(8,128)} fusion(f32[1024,6,64]{0,2,1:T(8,128)} %get-tuple-element.793, f32[6,512,1024]{2,1,0:T(8,128)} %get-tuple-element.730, pred[]{:T(512)S(6)} %compare.3, bf16[1024,6,64]{0,2,1:T(8,128)(2,1)S(1)} %copy-done.2, s32[]{:T(128)S(6)} %select_n.675), kind=kOutput, calls=%fused_computation.22.clone.1 | convolution fusion | flops 406585344 | bytes 16121861 | tf_op jit(solution)/shard_map/while/body/eval_jaxpr/hqk,qhd->khd/dot_general | solution.py:263
  314.1 8.9 %constant_dynamic-update-slice_fusion.2 = (bf16[6,1024,1024]{2,1,0:T(8,128)(2,1)}, bf16[6,512,1024]{2,1,0:T(8,128)(2,1)S(1)}) fusion(bf16[6,1024,1024]{2,1,0:T(8,128)(2,1)} %get-tuple-element.790, s32[]{:T(128)S(6)} %select_n.675, f32[6,512,1024]{2,1,0:T(8,128)} %get-tuple-element.730, f32[6,512,1024]{2,1,0:T(8,128)S(1)} %fusion.181, ...), kind=kLoop, calls=%fused_computation.35.clone.1 | loop fusion | flops 9437184 | bytes 37761028 | tf_op jit(solution)/shard_map/while/body/eval_jaxpr/dynamic_update_slice | solution.py:254
  330.4 9.6 %multiply_reduce_fusion.6 = (f32[6,512]{1,0:T(8,128)S(1)}, f32[6,512,1024]{2,1,0:T(8,128)}) fusion(f32[6,512,1024]{2,1,0:T(8,128)S(1)} %fusion.181, f32[6,512]{1,0:T(8,128)S(1)} %dynamic-slice_bitcast_fusion.15, bf16[6,1024,1024]{2,1,0:T(8,128)(2,1)} %get-tuple-element.812, s32[]{:T(128)S(6)} %select_n.675, ...), kind=kOutput, calls=%fused_computation.18.clone.1 | convolution fusion | flops 424670208 | bytes 32667648 | tf_op jit(solution)/shard_map/while/body/eval_jaxpr/qhd,khd->hqk/dot_general | solution.py:145
  340.0 7.4 %bitcast_add_fusion.6 = f32[1024,6,64]{0,2,1:T(8,128)} fusion(f32[1024,6,64]{0,2,1:T(8,128)} %get-tuple-element.793, f32[6,512,1024]{2,1,0:T(8,128)} %get-tuple-element.730, pred[]{:T(512)S(6)} %compare.3, bf16[1024,6,64]{0,2,1:T(8,128)(2,1)S(1)} %copy-done.2, s32[]{:T(128)S(6)} %select_n.675), kind=kOutput, calls=%fused_computation.22.clone.1 | convolution fusion | flops 406585344 | bytes 16121861 | tf_op jit(solution)/shard_map/while/body/eval_jaxpr/hqk,qhd->khd/dot_general | solution.py:263
  347.4 8.9 %constant_dynamic-update-slice_fusion.2 = (bf16[6,1024,1024]{2,1,0:T(8,128)(2,1)}, bf16[6,512,1024]{2,1,0:T(8,128)(2,1)S(1)}) fusion(bf16[6,1024,1024]{2,1,0:T(8,128)(2,1)} %get-tuple-element.790, s32[]{:T(128)S(6)} %select_n.675, f32[6,512,1024]{2,1,0:T(8,128)} %get-tuple-element.730, f32[6,512,1024]{2,1,0:T(8,128)S(1)} %fusion.181, ...), kind=kLoop, calls=%fused_computation.35.clone.1 | loop fusion | flops 9437184 | bytes 37761028 | tf_op jit(solution)/shard_map/while/body/eval_jaxpr/dynamic_update_slice | solution.py:254
  379.3 4.3 collective-permute-done.30
  400.4 4.3 collective-permute-done.25
  417.0 5.2 %collective-permute-done.27 = bf16[1,48,1152]{2,1,0:T(8,128)(2,1)S(1)} collective-permute-done((bf16[1,48,1152]{2,1,0:T(8,128)(2,1)S(1)}, bf16[1,48,1152]{2,1,0:T(8,128)(2,1)S(1)}, u32[]{:S(2)}, u32[]{:S(2)}) %collective-permute-start.27) | collective-permute-done | bytes 110624 | tf_op jit(solution)/shard_map/ppermute | solution.py:40
  426.8 15.9 %collective-permute-done.36 = bf16[8,48,1536]{2,1,0:T(8,128)(2,1)S(1)} collective-permute-done((bf16[8,48,1536]{2,1,0:T(8,128)(2,1)S(1)}, bf16[8,48,1536]{2,1,0:T(8,128)(2,1)S(1)}, u32[]{:S(2)}, u32[]{:S(2)}) %collective-permute-start.36) | collective-permute-done | bytes 1179680 | tf_op jit(solution)/shard_map/ppermute | solution.py:40
  447.3 17.7 %collective-permute-done.42 = bf16[8,192,384]{2,1,0:T(8,128)(2,1)} collective-permute-done((bf16[8,192,384]{2,1,0:T(8,128)(2,1)S(1)}, bf16[8,192,384]{2,1,0:T(8,128)(2,1)}, u32[]{:S(2)}, u32[]{:S(2)}) %collective-permute-start.42) | collective-permute-done | bytes 1179680 | tf_op jit(solution)/shard_map/ppermute | solution.py:40
  471.0 6.0 %collective-permute-done.43 = bf16[4,192,384]{2,1,0:T(8,128)(2,1)S(1)} collective-permute-done((bf16[4,192,384]{2,1,0:T(8,128)(2,1)S(1)}, bf16[4,192,384]{2,1,0:T(8,128)(2,1)S(1)}, u32[]{:S(2)}, u32[]{:S(2)}) %collective-permute-start.43) | collective-permute-done | bytes 589856 | tf_op jit(solution)/shard_map/ppermute | solution.py:40
  (456 shorter events, 240.5 us)
Async XLA Ops:
  6.8 13.8 %collective-permute-start.5 = (bf16[1,1,576]{2,1,0:T(2,128)(2,1)S(1)}, bf16[1,1,576]{2,1,0:T(2,128)(2,1)S(1)}, u32[]{:S(2)}, u32[]{:S(2)}) collective-permute-start(bf16[1,1,576]{2,1,0:T(2,128)(2,1)S(1)} %broadcast_in_dim_broadcast_in_dim.3), channel_id=1, source_target_pairs={{0,8},{1,9},{2,10},{3,11},{4,12},{5,13},{6,14},{7,15},{8,0},{9,1},... | collective-permute-start | bytes 3464 | tf_op jit(solution)/shard_map/ppermute | solution.py:40
  10.9 31.1 %collective-permute-start.10 = (bf16[1,48,768]{2,1,0:T(8,128)(2,1)}, bf16[1,48,768]{2,1,0:T(8,128)(2,1)S(1)}, u32[]{:S(2)}, u32[]{:S(2)}) collective-permute-start(bf16[1,48,768]{2,1,0:T(8,128)(2,1)} %bitcast.477), channel_id=1, source_target_pairs={{0,8},{1,9},{2,10},{3,11},{4,12},{5,13},{6,14},{7,15},{8,0},{9,1},... | collective-permute-start | bytes 221192 | tf_op jit(solution)/shard_map/ppermute | solution.py:40
  12.8 31.8 %collective-permute-start.1 = (bf16[1,48,1152]{2,1,0:T(8,128)(2,1)S(1)}, bf16[1,48,1152]{2,1,0:T(8,128)(2,1)S(1)}, u32[]{:S(2)}, u32[]{:S(2)}) collective-permute-start(bf16[1,48,1152]{2,1,0:T(8,128)(2,1)S(1)} %broadcast_in_dim_reshape.3), channel_id=1, source_target_pairs={{0,8},{1,9},{2,10},{3,11},{4,12},{5,13},{6,14},{7,15},{8,0},{9,1},... | collective-permute-start | bytes 331784 | tf_op jit(solution)/shard_map/ppermute | solution.py:40
  15.7 36.7 %collective-permute-start.18 = (bf16[1,192,768]{2,1,0:T(8,128)(2,1)}, bf16[1,192,768]{2,1,0:T(8,128)(2,1)S(1)}, u32[]{:S(2)}, u32[]{:S(2)}) collective-permute-start(bf16[1,192,768]{2,1,0:T(8,128)(2,1)} %bitcast.475), channel_id=1, source_target_pairs={{0,8},{1,9},{2,10},{3,11},{4,12},{5,13},{6,14},{7,15},{8,0},{9,1},... | collective-permute-start | bytes 884744 | tf_op jit(solution)/shard_map/ppermute | solution.py:40
  15.8 37.3 %collective-permute-start.14 = (bf16[1,48,3072]{2,1,0:T(8,128)(2,1)}, bf16[1,48,3072]{2,1,0:T(8,128)(2,1)S(1)}, u32[]{:S(2)}, u32[]{:S(2)}) collective-permute-start(bf16[1,48,3072]{2,1,0:T(8,128)(2,1)} %bitcast.476), channel_id=1, source_target_pairs={{0,8},{1,9},{2,10},{3,11},{4,12},{5,13},{6,14},{7,15},{8,0},{9,1},... | collective-permute-start | bytes 884744 | tf_op jit(solution)/shard_map/ppermute | solution.py:40
  20.6 9.7 %collective-permute-start.6 = (bf16[2,1,576]{2,0,1:T(2,128)(2,1)S(1)}, bf16[2,1,576]{2,0,1:T(2,128)(2,1)S(1)}, u32[]{:S(2)}, u32[]{:S(2)}) collective-permute-start(bf16[2,1,576]{2,0,1:T(2,128)(2,1)S(1)} %maximum_bitcast_fusion.4), channel_id=1, source_target_pairs={{0,4},{1,5},{2,6},{3,7},{4,0},{5,1},{6,2},{7,3},{8,12},{9,13},{10,... | collective-permute-start | bytes 6920 | tf_op jit(solution)/shard_map/ppermute | solution.py:40
  35.3 34.4 %collective-permute-start = (bf16[512,768]{1,0:T(8,128)(2,1)S(1)}, bf16[512,768]{1,0:T(8,128)(2,1)}, u32[]{:S(2)}, u32[]{:S(2)}) collective-permute-start(bf16[512,768]{1,0:T(8,128)(2,1)S(1)} %bitcast.472), channel_id=1, source_target_pairs={{0,16},{16,0},{1,17},{17,1},{2,18},{18,2},{3,19},{19,3},{4,20},{20... | collective-permute-start | bytes 2359304 | tf_op jit(solution)/shard_map/ppermute | solution.py:40
  44.6 10.9 %collective-permute-start.2 = (bf16[2,48,1152]{2,1,0:T(8,128)(2,1)S(1)}, bf16[2,48,1152]{2,1,0:T(8,128)(2,1)S(1)}, u32[]{:S(2)}, u32[]{:S(2)}) collective-permute-start(bf16[2,48,1152]{2,1,0:T(8,128)(2,1)S(1)} %maximum_bitcast_fusion.2), channel_id=1, source_target_pairs={{0,4},{1,5},{2,6},{3,7},{4,0},{5,1},{6,2},{7,3},{8,12},{9,13},{10,... | collective-permute-start | bytes 663560 | tf_op jit(solution)/shard_map/ppermute | solution.py:40
  50.8 9.9 %collective-permute-start.12 = (bf16[4,48,768]{2,1,0:T(8,128)(2,1)S(1)}, bf16[4,48,768]{2,1,0:T(8,128)(2,1)S(1)}, u32[]{:S(2)}, u32[]{:S(2)}) collective-permute-start(bf16[4,48,768]{2,1,0:T(8,128)(2,1)S(1)} %bitcast.469), channel_id=1, source_target_pairs={{0,2},{1,3},{2,0},{3,1},{4,6},{5,7},{6,4},{7,5},{8,10},{9,11},{10,... | collective-permute-start | bytes 884744 | tf_op jit(solution)/shard_map/ppermute | solution.py:40
  52.5 30.0 %collective-permute-start.19 = (bf16[2,192,768]{2,1,0:T(8,128)(2,1)S(1)}, bf16[2,192,768]{2,1,0:T(8,128)(2,1)S(1)}, u32[]{:S(2)}, u32[]{:S(2)}) collective-permute-start(bf16[2,192,768]{2,1,0:T(8,128)(2,1)S(1)} %maximum_bitcast_fusion.1), channel_id=1, source_target_pairs={{0,4},{1,5},{2,6},{3,7},{4,0},{5,1},{6,2},{7,3},{8,12},{9,13},{10,... | collective-permute-start | bytes 1769480 | tf_op jit(solution)/shard_map/ppermute | solution.py:40
  55.7 13.7 %collective-permute-start.3 = (bf16[4,48,1152]{2,1,0:T(8,128)(2,1)S(1)}, bf16[4,48,1152]{2,1,0:T(8,128)(2,1)S(1)}, u32[]{:S(2)}, u32[]{:S(2)}) collective-permute-start(bf16[4,48,1152]{2,1,0:T(8,128)(2,1)S(1)} %bitcast.462), channel_id=1, source_target_pairs={{0,2},{1,3},{2,0},{3,1},{4,6},{5,7},{6,4},{7,5},{8,10},{9,11},{10,... | collective-permute-start | bytes 1327112 | tf_op jit(solution)/shard_map/ppermute | solution.py:40
  57.3 23.4 %collective-permute-start.15 = (bf16[2,48,3072]{2,1,0:T(8,128)(2,1)S(1)}, bf16[2,48,3072]{2,1,0:T(8,128)(2,1)S(1)}, u32[]{:S(2)}, u32[]{:S(2)}) collective-permute-start(bf16[2,48,3072]{2,1,0:T(8,128)(2,1)S(1)} %maximum_bitcast_fusion), channel_id=1, source_target_pairs={{0,4},{1,5},{2,6},{3,7},{4,0},{5,1},{6,2},{7,3},{8,12},{9,13},{10,... | collective-permute-start | bytes 1769480 | tf_op jit(solution)/shard_map/ppermute | solution.py:40
  61.0 23.3 %collective-permute-start.13 = (bf16[8,48,768]{2,1,0:T(8,128)(2,1)S(1)}, bf16[8,48,768]{2,1,0:T(8,128)(2,1)S(1)}, u32[]{:S(2)}, u32[]{:S(2)}) collective-permute-start(bf16[8,48,768]{2,1,0:T(8,128)(2,1)S(1)} %bitcast.451), channel_id=1, source_target_pairs={{0,1},{1,0},{2,3},{3,2},{4,5},{5,4},{6,7},{7,6},{8,9},{9,8},{10,11... | collective-permute-start | bytes 1769480 | tf_op jit(solution)/shard_map/ppermute | solution.py:40
  69.7 15.7 %collective-permute-start.4 = (bf16[8,48,1152]{2,1,0:T(8,128)(2,1)S(1)}, bf16[8,48,1152]{2,1,0:T(8,128)(2,1)S(1)}, u32[]{:S(2)}, u32[]{:S(2)}) collective-permute-start(bf16[8,48,1152]{2,1,0:T(8,128)(2,1)S(1)} %bitcast.441), channel_id=1, source_target_pairs={{0,1},{1,0},{2,3},{3,2},{4,5},{5,4},{6,7},{7,6},{8,9},{9,8},{10,11... | collective-permute-start | bytes 2654216 | tf_op jit(solution)/shard_map/ppermute | solution.py:40
  80.9 29.0 %collective-permute-start.16 = (bf16[4,48,3072]{2,1,0:T(8,128)(2,1)S(1)}, bf16[4,48,3072]{2,1,0:T(8,128)(2,1)}, u32[]{:S(2)}, u32[]{:S(2)}) collective-permute-start(bf16[4,48,3072]{2,1,0:T(8,128)(2,1)S(1)} %bitcast.430), channel_id=1, source_target_pairs={{0,2},{1,3},{2,0},{3,1},{4,6},{5,7},{6,4},{7,5},{8,10},{9,11},{10,... | collective-permute-start | bytes 3538952 | tf_op jit(solution)/shard_map/ppermute | solution.py:40
  83.8 50.3 %collective-permute-start.20 = (bf16[4,192,768]{2,1,0:T(8,128)(2,1)}, bf16[4,192,768]{2,1,0:T(8,128)(2,1)}, u32[]{:S(2)}, u32[]{:S(2)}) collective-permute-start(bf16[4,192,768]{2,1,0:T(8,128)(2,1)} %bitcast.66), channel_id=1, source_target_pairs={{0,2},{1,3},{2,0},{3,1},{4,6},{5,7},{6,4},{7,5},{8,10},{9,11},{10,... | collective-permute-start | bytes 3538952 | tf_op jit(solution)/shard_map/ppermute | solution.py:40
  137.7 51.4 %collective-permute-start.21 = (bf16[8,192,768]{2,1,0:T(8,128)(2,1)}, bf16[8,192,768]{2,1,0:T(8,128)(2,1)}, u32[]{:S(2)}, u32[]{:S(2)}) collective-permute-start(bf16[8,192,768]{2,1,0:T(8,128)(2,1)} %bitcast.69), channel_id=1, source_target_pairs={{0,1},{1,0},{2,3},{3,2},{4,5},{5,4},{6,7},{7,6},{8,9},{9,8},{10,11... | collective-permute-start | bytes 7077896 | tf_op jit(solution)/shard_map/ppermute | solution.py:40
  137.7 54.9 %collective-permute-start.17 = (bf16[8,48,3072]{2,1,0:T(8,128)(2,1)}, bf16[8,48,3072]{2,1,0:T(8,128)(2,1)}, u32[]{:S(2)}, u32[]{:S(2)}) collective-permute-start(bf16[8,48,3072]{2,1,0:T(8,128)(2,1)} %bitcast.55), channel_id=1, source_target_pairs={{0,1},{1,0},{2,3},{3,2},{4,5},{5,4},{6,7},{7,6},{8,9},{9,8},{10,11... | collective-permute-start | bytes 7077896 | tf_op jit(solution)/shard_map/ppermute | solution.py:40
  176.6 11.1 %collective-permute-start.9 = (bf16[512,384]{0,1:T(8,128)(2,1)S(1)}, bf16[512,384]{0,1:T(8,128)(2,1)S(1)}, u32[]{:S(2)}, u32[]{:S(2)}) collective-permute-start(bf16[512,384]{0,1:T(8,128)(2,1)S(1)} %fusion.58), channel_id=1, source_target_pairs={{0,16},{16,0},{1,17},{17,1},{2,18},{18,2},{3,19},{19,3},{4,20},{20... | collective-permute-start | bytes 1179656 | tf_op jit(solution)/shard_map/ppermute | solution.py:40
  267.7 16.9 %collective-permute-start.22 = (bf16[512,384]{1,0:T(8,128)(2,1)S(1)}, bf16[512,384]{1,0:T(8,128)(2,1)S(1)}, u32[]{:S(2)}, u32[]{:S(2)}) collective-permute-start(bf16[512,384]{1,0:T(8,128)(2,1)S(1)} %constant_dynamic-slice_fusion.23), channel_id=1, source_target_pairs={{0,16},{16,0},{1,17},{17,1},{2,18},{18,2},{3,19},{19,3},{4,20},{20... | collective-permute-start | bytes 1179656 | tf_op jit(solution)/shard_map/ppermute | solution.py:40
  270.6 103.5 %collective-permute-start.29 = (bf16[8,48,768]{2,1,0:T(8,128)(2,1)}, bf16[8,48,768]{2,1,0:T(8,128)(2,1)}, u32[]{:S(2)}, u32[]{:S(2)}) collective-permute-start(bf16[8,48,768]{2,1,0:T(8,128)(2,1)} %dynamic-slice_bitcast_fusion.6), channel_id=1, source_target_pairs={{0,1},{1,0},{2,3},{3,2},{4,5},{5,4},{6,7},{7,6},{8,9},{9,8},{10,11... | collective-permute-start | bytes 1769480 | tf_op jit(solution)/shard_map/ppermute | solution.py:40
  281.1 130.0 %collective-permute-start.35 = (bf16[8,48,3072]{2,1,0:T(8,128)(2,1)}, bf16[8,48,3072]{2,1,0:T(8,128)(2,1)}, u32[]{:S(2)}, u32[]{:S(2)}) collective-permute-start(bf16[8,48,3072]{2,1,0:T(8,128)(2,1)} %dynamic-slice_bitcast_fusion.2), channel_id=1, source_target_pairs={{0,1},{1,0},{2,3},{3,2},{4,5},{5,4},{6,7},{7,6},{8,9},{9,8},{10,11... | collective-permute-start | bytes 7077896 | tf_op jit(solution)/shard_map/ppermute | solution.py:40
  281.1 141.9 %collective-permute-start.41 = (bf16[8,192,768]{2,1,0:T(8,128)(2,1)}, bf16[8,192,768]{2,1,0:T(8,128)(2,1)}, u32[]{:S(2)}, u32[]{:S(2)}) collective-permute-start(bf16[8,192,768]{2,1,0:T(8,128)(2,1)} %dynamic-slice_bitcast_fusion.1), channel_id=1, source_target_pairs={{0,1},{1,0},{2,3},{3,2},{4,5},{5,4},{6,7},{7,6},{8,9},{9,8},{10,11... | collective-permute-start | bytes 7077896 | tf_op jit(solution)/shard_map/ppermute | solution.py:40
  372.3 23.7 %collective-permute-start.24 = (bf16[8,48,1152]{2,1,0:T(8,128)(2,1)S(1)}, bf16[8,48,1152]{2,1,0:T(8,128)(2,1)S(1)}, u32[]{:S(2)}, u32[]{:S(2)}) collective-permute-start(bf16[8,48,1152]{2,1,0:T(8,128)(2,1)S(1)} %dynamic-slice_bitcast_fusion.3), channel_id=1, source_target_pairs={{0,1},{1,0},{2,3},{3,2},{4,5},{5,4},{6,7},{7,6},{8,9},{9,8},{10,11... | collective-permute-start | bytes 2654216 | tf_op jit(solution)/shard_map/ppermute | solution.py:40
  392.1 16.6 %collective-permute-start.23 = (bf16[512,768]{1,0:T(8,128)(2,1)S(1)}, bf16[512,768]{1,0:T(8,128)(2,1)S(1)}, u32[]{:S(2)}, u32[]{:S(2)}) collective-permute-start(bf16[512,768]{1,0:T(8,128)(2,1)S(1)} %fusion.54), channel_id=1, source_target_pairs={{0,16},{16,0},{1,17},{17,1},{2,18},{18,2},{3,19},{19,3},{4,20},{20... | collective-permute-start | bytes 2359304 | tf_op jit(solution)/shard_map/ppermute | solution.py:40
  398.7 17.6 %collective-permute-start.34 = (bf16[48,384]{1,0:T(8,128)(2,1)S(1)}, bf16[48,384]{1,0:T(8,128)(2,1)S(1)}, u32[]{:S(2)}, u32[]{:S(2)}) collective-permute-start(bf16[48,384]{1,0:T(8,128)(2,1)S(1)} %fusion.84), channel_id=1, source_target_pairs={{0,16},{16,0},{1,17},{17,1},{2,18},{18,2},{3,19},{19,3},{4,20},{20... | collective-permute-start | bytes 110600 | tf_op jit(solution)/shard_map/ppermute | solution.py:40
  413.8 28.9 %collective-permute-start.36 = (bf16[8,48,1536]{2,1,0:T(8,128)(2,1)S(1)}, bf16[8,48,1536]{2,1,0:T(8,128)(2,1)S(1)}, u32[]{:S(2)}, u32[]{:S(2)}) collective-permute-start(bf16[8,48,1536]{2,1,0:T(8,128)(2,1)S(1)} %constant_dynamic-slice_fusion.19), channel_id=1, source_target_pairs={{0,16},{16,0},{1,17},{17,1},{2,18},{18,2},{3,19},{19,3},{4,20},{20... | collective-permute-start | bytes 3538952 | tf_op jit(solution)/shard_map/ppermute | solution.py:40
  422.2 23.5 %collective-permute-start.28 = (bf16[48,1152]{1,0:T(8,128)(2,1)S(1)}, bf16[48,1152]{1,0:T(8,128)(2,1)S(1)}, u32[]{:S(2)}, u32[]{:S(2)}) collective-permute-start(bf16[48,1152]{1,0:T(8,128)(2,1)S(1)} %fusion.82), channel_id=1, source_target_pairs={{0,16},{16,0},{1,17},{17,1},{2,18},{18,2},{3,19},{19,3},{4,20},{20... | collective-permute-start | bytes 331784 | tf_op jit(solution)/shard_map/ppermute | solution.py:40
  425.3 39.6 %collective-permute-start.42 = (bf16[8,192,384]{2,1,0:T(8,128)(2,1)S(1)}, bf16[8,192,384]{2,1,0:T(8,128)(2,1)}, u32[]{:S(2)}, u32[]{:S(2)}) collective-permute-start(bf16[8,192,384]{2,1,0:T(8,128)(2,1)S(1)} %constant_dynamic-slice_fusion.17), channel_id=1, source_target_pairs={{0,16},{16,0},{1,17},{17,1},{2,18},{18,2},{3,19},{19,3},{4,20},{20... | collective-permute-start | bytes 3538952 | tf_op jit(solution)/shard_map/ppermute | solution.py:40
  444.0 24.8 %collective-permute-start.37 = (bf16[4,48,1536]{2,1,0:T(8,128)(2,1)}, bf16[4,48,1536]{2,1,0:T(8,128)(2,1)}, u32[]{:S(2)}, u32[]{:S(2)}) collective-permute-start(bf16[4,48,1536]{2,1,0:T(8,128)(2,1)} %dynamic-slice_bitcast_fusion.5), channel_id=1, source_target_pairs={{0,2},{1,3},{2,0},{3,1},{4,6},{5,7},{6,4},{7,5},{8,10},{9,11},{10,... | collective-permute-start | bytes 1769480 | tf_op jit(solution)/shard_map/ppermute | solution.py:40
  467.0 9.9 %collective-permute-start.43 = (bf16[4,192,384]{2,1,0:T(8,128)(2,1)S(1)}, bf16[4,192,384]{2,1,0:T(8,128)(2,1)S(1)}, u32[]{:S(2)}, u32[]{:S(2)}) collective-permute-start(bf16[4,192,384]{2,1,0:T(8,128)(2,1)S(1)} %dynamic-slice_bitcast_fusion.4), channel_id=1, source_target_pairs={{0,2},{1,3},{2,0},{3,1},{4,6},{5,7},{6,4},{7,5},{8,10},{9,11},{10,... | collective-permute-start | bytes 1769480 | tf_op jit(solution)/shard_map/ppermute | solution.py:40
  470.0 11.1 %collective-permute-start.38 = (bf16[2,48,1536]{2,1,0:T(8,128)(2,1)S(1)}, bf16[2,48,1536]{2,1,0:T(8,128)(2,1)S(1)}, u32[]{:S(2)}, u32[]{:S(2)}) collective-permute-start(bf16[2,48,1536]{2,1,0:T(8,128)(2,1)S(1)} %dynamic-slice_bitcast_fusion.9), channel_id=1, source_target_pairs={{0,4},{1,5},{2,6},{3,7},{4,0},{5,1},{6,2},{7,3},{8,12},{9,13},{10,... | collective-permute-start | bytes 884744 | tf_op jit(solution)/shard_map/ppermute | solution.py:40
  (88 other events, 694.9 us)
